TPU v7x, 32 devices: a whole 2x2x4 slice. The times are simulated.
32 devices in a mesh: expert: 8 (over z, x), tensor: 4 (over y, core).
Axes of the slice: x: 2, y: 2, z: 4, core: 2. Of those that a mesh axis runs over, the one named last changes fastest.
Arguments:
- hidden_in: bfloat16 [4096, 2048], P('expert'), may hold values from -6 to 6
- doc_ids: int32 [8, 512], P('expert'), may hold values from 0 to 2, never falling along the last dimension, each value on 1 to 384 neighbouring positions
- routes: int32 [4096, 8], P('expert'), may hold values from 0 to 15, all different within a row
- out_grad: bfloat16 [4096, 2048], P('expert'), may hold values from -6 to 6
- norm1_gain: float32 [2048], replicated, may hold values from 0.5 to 1.5
- q_weight: bfloat16 [2048, 2048], P(None, 'tensor'), may hold values from -0.125 to 0.125
- k_weight: bfloat16 [2048, 2048], P(None, 'tensor'), may hold values from -0.125 to 0.125
- v_weight: bfloat16 [2048, 2048], P(None, 'tensor'), may hold values from -0.125 to 0.125
- o_weight: bfloat16 [2048, 2048], P(None, 'tensor'), may hold values from -1.5 to 1.5
- q_gain: float32 [128], replicated, may hold values from 0.5 to 1.5
- k_gain: float32 [128], replicated, may hold values from 0.5 to 1.5
- norm2_gain: float32 [2048], replicated, may hold values from 0.5 to 1.5
- router_weight: bfloat16 [2048, 16], replicated, may hold values from -0.0625 to 0.0625
- gate_weight: bfloat16 [16, 2048, 1024], P('expert', None, 'tensor'), may hold values from -0.125 to 0.125
- up_weight: bfloat16 [16, 2048, 1024], P('expert', None, 'tensor'), may hold values from -0.125 to 0.125
- down_weight: bfloat16 [16, 1024, 2048], P('expert', 'tensor'), may hold values from -0.5 to 0.5
Outputs:
- output: bfloat16 [4096, 2048], P('expert')
- input_grad: float32 [4096, 2048], P('expert')
- norm1_gain_grad: float32 [2048], P('expert')
- q_weight_grad: float32 [2048, 2048], P('expert', 'tensor')
- k_weight_grad: float32 [2048, 2048], P('expert', 'tensor')
- v_weight_grad: float32 [2048, 2048], P('expert', 'tensor')
- o_weight_grad: float32 [2048, 2048], P('expert', 'tensor')
- q_gain_grad: float32 [128], P('expert')
- k_gain_grad: float32 [128], P('expert')
- norm2_gain_grad: float32 [2048], P('expert')
- router_weight_grad: float32 [2048, 16], P('expert')
- gate_weight_grad: float32 [16, 2048, 1024], P('expert', None, 'tensor')
- up_weight_grad: float32 [16, 2048, 1024], P('expert', None, 'tensor')
- down_weight_grad: float32 [16, 1024, 2048], P('expert', 'tensor')
Inputs may be any that keep to these rules, and one draw needn't show every extreme that they name: Each row of routes names 8 different experts. `doc_ids`: within a packed row ids never fall; a document has at most 384 tokens.
All inputs are finite; a program needn't handle non-finite values.
Results may differ from a plain program's by a relative error of at most 0.024.
Values may be sent and summed in bfloat16 or wider, within the bound.
No kernel may reach another device: no remote copies, remote signals or barrier semaphores. Data moves between devices by JAX's collectives and lax.ppermute only.
A program may use at most 320 MiB of HBM per device.

v0:
```python
import jax
import jax.numpy as jnp
from jax import lax
from jax.sharding import PartitionSpec as P

epsilon = 1e-06
rope_base = 10000.0
masked_score = -1e30


def rms_scale(values):
    return lax.rsqrt(jnp.mean(values * values, axis=-1, keepdims=True) + epsilon)


def rotary(positions, head_size):
    half_size = head_size // 2
    freqs = rope_base ** (-2.0 * jnp.arange(half_size, dtype=jnp.float32) / head_size)
    angles = jnp.arange(positions, dtype=jnp.float32)[:, None] * freqs[None, :]
    cosine = jnp.cos(angles)
    sine = jnp.sin(angles)
    return (jnp.concatenate([cosine, cosine], -1), jnp.concatenate([sine, sine], -1))


def prep_heads(raw, gain, factor, cosine, sine, heads):
    shaped = raw.reshape(raw.shape[0], heads, -1)
    normed = shaped * rms_scale(shaped) * gain
    half_size = normed.shape[-1] // 2
    turned = jnp.concatenate([-normed[..., half_size:], normed[..., :half_size]], -1)
    return (normed * cosine[:, None, :] + turned * sine[:, None, :]) * factor


def slot_tables(route_rows, all_experts, capacity):
    num_tokens, num_picks = route_rows.shape
    flat_routes = route_rows.reshape(-1)
    onehot = (flat_routes[:, None] == jnp.arange(all_experts, dtype=jnp.int32)[None, :]).astype(
        jnp.int32
    )
    before = jnp.cumsum(onehot, axis=0) - onehot
    placed = jnp.sum(before * onehot, axis=1)
    slot_ids = jnp.where(placed < capacity, flat_routes * capacity + placed, all_experts * capacity)
    pair_ids = jnp.arange(num_tokens * num_picks, dtype=jnp.int32)
    pair_of = (
        jnp.full((all_experts * capacity + 1,), num_tokens * num_picks, jnp.int32)
        .at[slot_ids]
        .set(pair_ids)
    )
    return (slot_ids.reshape(num_tokens, num_picks), pair_of[:-1])


def on_device(
    hidden_in,
    doc_ids,
    routes,
    out_grad,
    norm1_gain,
    q_weight,
    k_weight,
    v_weight,
    o_weight,
    q_gain,
    k_gain,
    norm2_gain,
    router_weight,
    gate_weight,
    up_weight,
    down_weight,
):
    num_tokens, model_width = hidden_in.shape
    num_picks = routes.shape[1]
    head_size = q_gain.shape[0]
    local_heads = q_weight.shape[1] // head_size
    local_experts = gate_weight.shape[0]
    ffn_local = gate_weight.shape[2]
    expert_ranks = lax.axis_size("expert")
    tensor_ranks = lax.axis_size("tensor")
    all_experts = local_experts * expert_ranks
    capacity = tensor_ranks * (
        (9 * num_tokens * num_picks + 8 * all_experts * tensor_ranks - 1)
        // (8 * all_experts * tensor_ranks)
    )
    doc_row = doc_ids[0]
    cosine, sine = rotary(num_tokens, head_size)
    zero_row = jnp.zeros((1, model_width), jnp.bfloat16)
    inputs = hidden_in.astype(jnp.float32)
    scale_one = rms_scale(inputs)
    unit_one = inputs * scale_one
    normed_one = (unit_one * norm1_gain).astype(jnp.bfloat16)
    q_raw = jnp.dot(normed_one, q_weight, preferred_element_type=jnp.float32)
    k_raw = jnp.dot(normed_one, k_weight, preferred_element_type=jnp.float32)
    v_raw = jnp.dot(normed_one, v_weight, preferred_element_type=jnp.float32)

    def shape_heads(q_in, k_in, q_scale, k_scale):
        return (
            prep_heads(q_in, q_scale, head_size ** (-0.5), cosine, sine, local_heads),
            prep_heads(k_in, k_scale, 1.0, cosine, sine, local_heads),
        )

    head_vals, head_back = jax.vjp(shape_heads, q_raw, k_raw, q_gain, k_gain)
    queries = head_vals[0].astype(jnp.bfloat16)
    keys = head_vals[1].astype(jnp.bfloat16)
    values = v_raw.astype(jnp.bfloat16).reshape(num_tokens, local_heads, head_size)

    def block_scores():
        scores = jnp.einsum("qhd,khd->hqk", queries, keys, preferred_element_type=jnp.float32)
        return (
            jnp.where((doc_row[:, None] == doc_row[None, :])[None], scores, masked_score),
            queries,
        )

    scores, query_blk = block_scores()
    peak = jnp.max(scores, -1, keepdims=True)
    log_total = peak + jnp.log(jnp.sum(jnp.exp(scores - peak), -1, keepdims=True))
    weights = jnp.exp(scores - log_total).astype(jnp.bfloat16)
    block_outs = jnp.einsum("hqk,khd->qhd", weights, values, preferred_element_type=jnp.float32)
    attn_out = block_outs.reshape(num_tokens, local_heads * head_size).astype(jnp.bfloat16)
    attn_part = lax.dot_general(
        attn_out, o_weight, (((1,), (1,)), ((), ())), preferred_element_type=jnp.float32
    )
    attn_full = lax.psum(attn_part, "tensor")
    after_attn = inputs + attn_full
    scale_two = rms_scale(after_attn)
    unit_two = after_attn * scale_two
    normed_two = (unit_two * norm2_gain).astype(jnp.bfloat16)
    logits = jnp.dot(normed_two, router_weight, preferred_element_type=jnp.float32)
    pick_mask = routes[:, :, None] == jnp.arange(all_experts, dtype=jnp.int32)[None, None, :]
    chosen = jnp.sum(jnp.where(pick_mask, logits[:, None, :], 0.0), -1)
    gates = jax.nn.softmax(chosen, -1)
    slot_ids, pair_of = slot_tables(routes, all_experts, capacity)
    owners = pair_of // num_picks
    padded_rows = jnp.concatenate([normed_two, zero_row], 0)
    send_buf = jnp.take(padded_rows, owners, axis=0).reshape(
        expert_ranks, local_experts, capacity, model_width
    )
    slot_rows = lax.all_to_all(send_buf, "expert", split_axis=0, concat_axis=0, tiled=True)
    gate_up = jnp.concatenate([gate_weight, up_weight], 2)
    joint_pre = jnp.einsum("secd,edf->secf", slot_rows, gate_up, preferred_element_type=jnp.float32)
    gate_pre = joint_pre[..., :ffn_local]
    up_pre = joint_pre[..., ffn_local:]
    silu_gate = jax.nn.silu(gate_pre)
    hidden = (silu_gate * up_pre).astype(jnp.bfloat16)
    partial_out = jnp.einsum(
        "secf,efd->secd", hidden, down_weight, preferred_element_type=jnp.float32
    ).astype(jnp.bfloat16)
    out_grads = out_grad.astype(jnp.float32)
    mixture = jnp.zeros((num_tokens, model_width), jnp.float32)
    gate_dots = []
    returned = lax.all_to_all(
        partial_out, "expert", split_axis=0, concat_axis=0, tiled=True
    ).reshape(all_experts * capacity, model_width)
    returned = jnp.concatenate([returned, zero_row], 0)
    for rank_k in range(num_picks):
        picked = jnp.take(returned, slot_ids[:, rank_k], axis=0)
        mixture = mixture + gates[:, rank_k, None] * picked
        gate_dots.append(jnp.sum(out_grads * picked, -1))
    moe_full = lax.psum(mixture.astype(jnp.bfloat16), "tensor").astype(jnp.float32)
    output = (after_attn + moe_full).astype(jnp.bfloat16)
    dgate_part = jnp.stack(gate_dots, -1)
    padded_gates = jnp.concatenate([gates.reshape(-1), jnp.zeros((1,), jnp.float32)], 0)
    padded_grads = jnp.concatenate([out_grads, jnp.zeros((1, model_width), jnp.float32)], 0)
    slot_gate = jnp.take(padded_gates, pair_of, axis=0)
    grad_buf = (slot_gate[:, None] * jnp.take(padded_grads, owners, axis=0)).astype(jnp.bfloat16)
    grads_in = lax.all_to_all(
        grad_buf.reshape(expert_ranks, local_experts, capacity, model_width),
        "expert",
        split_axis=0,
        concat_axis=0,
        tiled=True,
    )
    dhidden = jnp.einsum(
        "secd,efd->secf", grads_in, down_weight, preferred_element_type=jnp.float32
    )
    down_grad = jnp.einsum("secf,secd->efd", hidden, grads_in, preferred_element_type=jnp.float32)
    sig_gate = jax.nn.sigmoid(gate_pre)
    dgate_pre = dhidden * up_pre * (sig_gate * (1.0 + gate_pre * (1.0 - sig_gate)))
    dup_pre = dhidden * silu_gate
    djoint = jnp.concatenate([dgate_pre, dup_pre], -1).astype(jnp.bfloat16)
    joint_grad = jnp.einsum("secd,secf->edf", slot_rows, djoint, preferred_element_type=jnp.float32)
    gate_grad = joint_grad[..., :ffn_local]
    up_grad = joint_grad[..., ffn_local:]
    dslot_in = jnp.einsum(
        "secf,edf->secd", djoint, gate_up, preferred_element_type=jnp.float32
    ).astype(jnp.bfloat16)
    dnormed_part = jnp.zeros((num_tokens, model_width), jnp.float32)
    came_back = lax.all_to_all(dslot_in, "expert", split_axis=0, concat_axis=0, tiled=True).reshape(
        all_experts * capacity, model_width
    )
    came_back = jnp.concatenate([came_back, zero_row], 0)
    for rank_k in range(num_picks):
        dnormed_part = dnormed_part + jnp.take(came_back, slot_ids[:, rank_k], axis=0)
    dnormed_exp, dgate_all = lax.psum((dnormed_part, dgate_part), "tensor")
    dsel = gates * (dgate_all - jnp.sum(gates * dgate_all, -1, keepdims=True))
    dlogits = jnp.sum(jnp.where(pick_mask, dsel[:, :, None], 0.0), 1).astype(jnp.bfloat16)
    router_grad = lax.dot_general(
        normed_two, dlogits, (((0,), (0,)), ((), ())), preferred_element_type=jnp.float32
    )
    dnormed_two = dnormed_exp + lax.dot_general(
        dlogits, router_weight, (((1,), (1,)), ((), ())), preferred_element_type=jnp.float32
    )
    norm2_grad = jnp.sum(dnormed_two * unit_two, 0)
    weighted_two = dnormed_two * norm2_gain
    dafter = out_grads + scale_two * (
        weighted_two - unit_two * jnp.mean(weighted_two * unit_two, -1, keepdims=True)
    )
    dattn = dafter.astype(jnp.bfloat16)
    o_grad = lax.dot_general(
        dattn, attn_out, (((0,), (0,)), ((), ())), preferred_element_type=jnp.float32
    )
    dattn_out = (
        jnp.dot(dattn, o_weight, preferred_element_type=jnp.float32)
        .astype(jnp.bfloat16)
        .reshape(num_tokens, local_heads, head_size)
    )
    scores, query_blk = block_scores()
    probs = jnp.exp(scores - log_total)
    dprobs = jnp.einsum("qhd,khd->hqk", dattn_out, values, preferred_element_type=jnp.float32)
    dscores = (probs * (dprobs - jnp.sum(probs * dprobs, -1, keepdims=True))).astype(jnp.bfloat16)
    dquery_blocks = jnp.einsum("hqk,khd->qhd", dscores, keys, preferred_element_type=jnp.float32)
    dkey = jnp.einsum("hqk,qhd->khd", dscores, query_blk, preferred_element_type=jnp.float32)
    dvalue = jnp.einsum(
        "hqk,qhd->khd", probs.astype(jnp.bfloat16), dattn_out, preferred_element_type=jnp.float32
    )
    dq_raw, dk_raw, q_gain_part, k_gain_part = head_back((dquery_blocks, dkey))
    dq_low = dq_raw.astype(jnp.bfloat16)
    dk_low = dk_raw.astype(jnp.bfloat16)
    dv_low = dvalue.reshape(num_tokens, local_heads * head_size).astype(jnp.bfloat16)
    contract_rows = (((0,), (0,)), ((), ()))
    contract_cols = (((1,), (1,)), ((), ()))
    q_grad = lax.dot_general(normed_one, dq_low, contract_rows, preferred_element_type=jnp.float32)
    k_grad = lax.dot_general(normed_one, dk_low, contract_rows, preferred_element_type=jnp.float32)
    v_grad = lax.dot_general(normed_one, dv_low, contract_rows, preferred_element_type=jnp.float32)
    dnormed_one = lax.dot_general(
        dq_low, q_weight, contract_cols, preferred_element_type=jnp.float32
    )
    dnormed_one = dnormed_one + lax.dot_general(
        dk_low, k_weight, contract_cols, preferred_element_type=jnp.float32
    )
    dnormed_one = dnormed_one + lax.dot_general(
        dv_low, v_weight, contract_cols, preferred_element_type=jnp.float32
    )
    dnormed_full, q_gain_sum, k_gain_sum = (
        lax.psum(dnormed_one.astype(jnp.bfloat16), "tensor").astype(jnp.float32),
        lax.psum(q_gain_part.astype(jnp.bfloat16), "tensor").astype(jnp.float32),
        lax.psum(k_gain_part.astype(jnp.bfloat16), "tensor").astype(jnp.float32),
    )
    norm1_grad = jnp.sum(dnormed_full * unit_one, 0)
    weighted_one = dnormed_full * norm1_gain
    input_grad = dafter + scale_one * (
        weighted_one - unit_one * jnp.mean(weighted_one * unit_one, -1, keepdims=True)
    )
    reduced = (
        lax.psum_scatter(
            q_grad.astype(jnp.bfloat16), "expert", scatter_dimension=0, tiled=True
        ).astype(jnp.float32),
        lax.psum_scatter(
            k_grad.astype(jnp.bfloat16), "expert", scatter_dimension=0, tiled=True
        ).astype(jnp.float32),
        lax.psum_scatter(
            v_grad.astype(jnp.bfloat16), "expert", scatter_dimension=0, tiled=True
        ).astype(jnp.float32),
        lax.psum_scatter(
            o_grad.astype(jnp.bfloat16), "expert", scatter_dimension=0, tiled=True
        ).astype(jnp.float32),
        lax.psum_scatter(
            router_grad.astype(jnp.bfloat16), "expert", scatter_dimension=0, tiled=True
        ).astype(jnp.float32),
        lax.psum_scatter(
            norm1_grad.astype(jnp.bfloat16), "expert", scatter_dimension=0, tiled=True
        ).astype(jnp.float32),
        lax.psum_scatter(
            norm2_grad.astype(jnp.bfloat16), "expert", scatter_dimension=0, tiled=True
        ).astype(jnp.float32),
        lax.psum_scatter(
            q_gain_sum.astype(jnp.bfloat16), "expert", scatter_dimension=0, tiled=True
        ).astype(jnp.float32),
        lax.psum_scatter(
            k_gain_sum.astype(jnp.bfloat16), "expert", scatter_dimension=0, tiled=True
        ).astype(jnp.float32),
    )
    return (
        output,
        input_grad,
        reduced[5],
        reduced[0],
        reduced[1],
        reduced[2],
        reduced[3],
        reduced[7],
        reduced[8],
        reduced[6],
        reduced[4],
        gate_grad,
        up_grad,
        down_grad,
    )


def solution(mesh):
    return jax.shard_map(
        on_device,
        mesh=mesh,
        in_specs=(
            P("expert", None),
            P("expert", None),
            P("expert", None),
            P("expert", None),
            P(),
            P(None, "tensor"),
            P(None, "tensor"),
            P(None, "tensor"),
            P(None, "tensor"),
            P(),
            P(),
            P(),
            P(),
            P("expert", None, "tensor"),
            P("expert", None, "tensor"),
            P("expert", "tensor", None),
        ),
        out_specs=(
            P("expert", None),
            P("expert", None),
            P("expert"),
            P("expert", "tensor"),
            P("expert", "tensor"),
            P("expert", "tensor"),
            P("expert", "tensor"),
            P("expert"),
            P("expert"),
            P("expert"),
            P("expert", None),
            P("expert", None, "tensor"),
            P("expert", None, "tensor"),
            P("expert", "tensor", None),
        ),
        check_vma=False,
    )
```

profile of v0, /device:TPU:0, one launch (start us, length us, event | category | flops | bytes accessed | tf_op | source)
XLA Modules:
  0.0 2747.8 jit_solution(8802034476952752222)
XLA Ops:
  11.3 3.7 convolution_convert_fusion.6
  25.3 3.3 fusion.95
  29.7 5.0 reduce-window.6
  36.9 15.5 scatter_custom_fusion
  53.3 63.7 %all-reduce.19.cloned.1.call-done = f32[512,2048]{1,0:T(8,128)} async-done(((f32[512,2048]{1,0:T(8,128)}), f32[512,2048]{1,0:T(8,128)}) %all-reduce.19.cloned.1.call-update) | async-done | bytes 4194320 | tf_op jit(solution)/shard_map/psum | solution.py:119
  117.0 3.5 multiply_reduce_fusion.3
  124.1 36.9 %gather_fusion = bf16[4608,2048]{1,0:T(8,128)(2,1)} fusion(bf16[513,2048]{1,0:T(8,128)(2,1)} %concatenate.39, s32[5120]{0:T(1024)S(1)} %get-tuple-element.104), kind=kCustom, calls=%fused_computation.16 | custom fusion | bytes 37767168 | tf_op jit(solution)/shard_map/jit(_take)/gather | solution.py:131
  161.0 9.7 broadcast_select_fusion
  170.8 413.4 %all_to_all.20 = bf16[8,2,288,2048]{3,2,1,0:T(8,128)(2,1)} all-to-all(bf16[8,2,288,2048]{3,2,1,0:T(8,128)(2,1)S(1)} %broadcast_select_fusion), channel_id=1, replica_groups=mesh['expert'=8,'tensor'=4] {'expert'}, dimensions={0} | all-to-all | bytes 37748736 | tf_op jit(solution)/shard_map/all_to_all | solution.py:134
  584.2 16.5 fusion.42
  600.7 4.5 multiply_convert_fusion.1
  605.2 9.1 convert_bitcast_fusion.1
  614.3 16.9 copy.110
  631.2 5.9 all-to-all-start.1
  637.1 4.1 concatenate.42
  641.3 36.4 %gather_fusion.2 = f32[4608,2048]{1,0:T(8,128)} fusion(f32[513,2048]{1,0:T(8,128)} %concatenate.42, s32[5120]{0:T(1024)S(1)} %get-tuple-element.104), kind=kCustom, calls=%fused_computation.18 | custom fusion | bytes 75515904 | tf_op jit(solution)/shard_map/jit(_take)/gather | solution.py:161
  681.5 362.4 %all-to-all-done.1 = bf16[8,2,288,2048]{3,2,1,0:T(8,128)(2,1)} async-done(((bf16[8,2,288,2048]{3,2,1,0:T(8,128)(2,1)}), bf16[8,2,288,2048]{3,2,1,0:T(8,128)(2,1)}, u32[]{:S(2)}, u32[]{:S(2)}) %all-to-all-start.1) | async-done | bytes 18874400 | tf_op jit(solution)/shard_map/all_to_all | solution.py:147
  1044.0 16.9 concatenate.40
  1060.9 14.0 gather_fusion.10
  1074.9 14.2 gather_fusion.9
  1089.1 14.0 gather_fusion.8
  1103.2 14.4 gather_fusion.7
  1117.6 14.1 gather_fusion.6
  1131.7 14.1 gather_fusion.5
  1145.8 14.2 gather_fusion.4
  1160.0 14.0 gather_fusion.3
  1174.1 8.9 fusion.41
  1183.1 10.1 psum.52
  1194.1 24.1 gather_fusion.1
  1218.4 14.2 multiply_convert_fusion
  1232.6 412.0 %all_to_all.21 = bf16[8,2,288,2048]{3,2,1,0:T(8,128)(2,1)} all-to-all(bf16[8,2,288,2048]{3,2,1,0:T(8,128)(2,1)S(1)} %multiply_convert_fusion), channel_id=1, replica_groups=mesh['expert'=8,'tensor'=4] {'expert'}, dimensions={0} | all-to-all | bytes 37748736 | tf_op jit(solution)/shard_map/all_to_all | solution.py:162
  1644.6 14.0 fusion.12
  1658.6 15.6 convert_bitcast_fusion
  1674.2 9.3 copy.113
  1683.5 411.1 %all_to_all.22 = bf16[8,2,288,2048]{3,2,1,0:T(8,128)(2,1)S(1)} all-to-all(bf16[8,2,288,2048]{3,2,1,0:T(8,128)(2,1)S(1)} %copy.113), channel_id=1, replica_groups=mesh['expert'=8,'tensor'=4] {'expert'}, dimensions={0} | all-to-all | bytes 37748736 | tf_op jit(solution)/shard_map/all_to_all | solution.py:184
  2094.6 8.1 concatenate.44
  2102.7 13.2 gather_fusion.18
  2115.9 14.3 gather_fusion.17
  2130.2 14.0 gather_fusion.16
  2144.2 14.1 gather_fusion.15
  2158.3 14.3 gather_fusion.14
  2172.6 14.1 gather_fusion.13
  2186.7 14.4 gather_fusion.12
  2201.2 14.1 gather_fusion.11
  2215.3 8.4 convert_add_fusion.2
  2226.5 10.0 fusion.29
  2236.6 70.6 %all-reduce.21.cloned.1.call-done = f32[512,2048]{1,0:T(8,128)} async-done(((f32[512,2048]{1,0:T(8,128)}), f32[512,2048]{1,0:T(8,128)}) %all-reduce.21.cloned.1.call-update) | async-done | bytes 4194320 | tf_op jit(solution)/shard_map/psum | solution.py:190
  2307.2 4.9 multiply_reduce_fusion
  2333.0 4.9 convolution_convert_fusion
  2338.0 3.9 convolution_convert_fusion.1
  2343.9 21.3 reduce-scatter.14.cloned.1.call-done
  2369.4 17.9 fusion.17
  2390.2 11.3 fusion.45
  2401.5 51.8 %all-reduce.23.cloned.1.call-done = (bf16[512,2048]{1,0:T(8,128)(2,1)}, bf16[512,2048]{1,0:T(8,128)(2,1)}) async-done(((bf16[512,2048]{1,0:T(8,128)(2,1)}, bf16[512,2048]{1,0:T(8,128)(2,1)}), (bf16[512,2048]{1,0:T(8,128)(2,1)}, bf16[512,2048]{1,0:T(8,128)(2,1)})) %all-reduce.23.cloned.1.call-update) | async-done | bytes 4194320 | tf_op jit(solution)/shard_map/psum | solution.py:155
  2453.3 2.9 fusion.32
  2456.2 22.2 all-reduce.12
  2478.5 7.6 fusion.91
  2486.1 6.0 all-reduce.13
  2494.4 4.4 add_convert_fusion.1
  2500.0 3.3 fusion.21
  2503.3 22.2 reduce-scatter.12.cloned.1.call-done
  2527.3 69.3 %reduce-scatter.10.cloned.1.call-done = bf16[256,512]{1,0:T(8,128)(2,1)} async-done(((bf16[2048,512]{1,0:T(8,128)(2,1)}), bf16[256,512]{1,0:T(8,128)(2,1)}) %reduce-scatter.10.cloned.1.call-update) | async-done | bytes 262160 | tf_op jit(solution)/shard_map/reduce_scatter | solution.py:257
  2598.4 69.4 %reduce-scatter.6.cloned.1.call-done = bf16[256,512]{1,0:T(8,128)(2,1)} async-done(((bf16[2048,512]{1,0:T(8,128)(2,1)}), bf16[256,512]{1,0:T(8,128)(2,1)}) %reduce-scatter.6.cloned.1.call-update) | async-done | bytes 262160 | tf_op jit(solution)/shard_map/reduce_scatter | solution.py:251
  2669.6 69.2 %reduce-scatter.8.cloned.1.call-done = bf16[256,512]{1,0:T(8,128)(2,1)} async-done(((bf16[2048,512]{1,0:T(8,128)(2,1)}), bf16[256,512]{1,0:T(8,128)(2,1)}) %reduce-scatter.8.cloned.1.call-update) | async-done | bytes 262160 | tf_op jit(solution)/shard_map/reduce_scatter | solution.py:254
  (356 shorter events, 68.3 us)
Async XLA Ops:
  7.2 598.0 %copy-start = (bf16[2,256,2048]{2,1,0:T(8,128)(2,1)S(1)}, bf16[2,256,2048]{2,1,0:T(8,128)(2,1)}, u32[]{:S(2)}) copy-start(bf16[2,256,2048]{2,1,0:T(8,128)(2,1)} %param.33) | copy-start | bytes 6291460
  7.2 109.8 %all-reduce.19.cloned.1.call-start = ((), (), s32[]{:S(2)}) async-start(), calls=%async_computation.9 | async-start | bytes 8388608 | tf_op jit(solution)/shard_map/psum | solution.py:119
  9.5 7.6 copy-start.78
  11.3 11.8 copy-start.21
  15.0 8.0 copy-start.45
  52.6 67.9 %copy-start.52 = (s32[8,2,288]{2,1,0:T(2,128)}, s32[8,2,288]{2,1,0:T(2,128)S(1)}, u32[]{:S(2)}) copy-start(s32[8,2,288]{2,1,0:T(2,128)S(1)} %slice.99) | copy-start | bytes 55300
  53.3 107.7 %copy-start.63 = (pred[8,2,288]{2,1,0:T(4,128)(4,1)}, pred[8,2,288]{2,1,0:T(4,128)(4,1)S(1)}, u32[]{:S(2)}) copy-start(pred[8,2,288]{2,1,0:T(4,128)(4,1)S(1)} %compare_and_fusion) | copy-start | bytes 13828
  53.3 67.2 %copy-start.66 = (f32[2048]{0:T(1024)S(1)}, f32[2048]{0:T(1024)}, u32[]{:S(2)}) copy-start(f32[2048]{0:T(1024)} %param.29) | copy-start | bytes 24580
  605.2 9.1 copy-start.19
  631.2 412.7 %all-to-all-start.1 = ((bf16[8,2,288,2048]{3,2,1,0:T(8,128)(2,1)}), bf16[8,2,288,2048]{3,2,1,0:T(8,128)(2,1)}, u32[]{:S(2)}, u32[]{:S(2)}) async-start(bf16[8,2,288,2048]{3,2,1,0:T(8,128)(2,1)} %copy.110), calls=%async_computation.1 | async-start | bytes 37748736 | tf_op jit(solution)/shard_map/all_to_all | solution.py:147
  637.1 1670.1 %all-reduce.21.cloned.1.call-start = ((), (), s32[]{:S(2)}) async-start(), calls=%async_computation.10 | async-start | bytes 8388608 | tf_op jit(solution)/shard_map/psum | solution.py:190
  641.3 36.4 %copy-start.13 = (s32[512,8]{1,0:T(8,128)S(1)}, s32[512,8]{1,0:T(8,128)}, u32[]{:S(2)}) copy-start(s32[512,8]{1,0:T(8,128)} %get-tuple-element.67) | copy-start | bytes 49156
  641.3 37.9 %copy-start.48 = (bf16[2048,16]{0,1:T(8,128)(2,1)S(1)}, bf16[2048,16]{0,1:T(8,128)(2,1)}, u32[]{:S(2)}) copy-start(bf16[2048,16]{0,1:T(8,128)(2,1)} %param.30) | copy-start | bytes 196612
  678.8 467.0 %copy-start.80 = (s32[1024]{0:T(1024)}, s32[1024]{0:T(1024)S(1)}, u32[]{:S(2)}) copy-start(s32[1024]{0:T(1024)S(1)} %pad_clamp_fusion.8) | copy-start | bytes 12292
  678.8 438.8 %copy-start.82 = (s32[1024]{0:T(1024)}, s32[1024]{0:T(1024)S(1)}, u32[]{:S(2)}) copy-start(s32[1024]{0:T(1024)S(1)} %pad_clamp_fusion.6) | copy-start | bytes 12292
  678.9 410.3 %copy-start.86 = (s32[1024]{0:T(1024)}, s32[1024]{0:T(1024)S(1)}, u32[]{:S(2)}) copy-start(s32[1024]{0:T(1024)S(1)} %pad_clamp_fusion.4) | copy-start | bytes 12292
  678.9 382.0 %copy-start.90 = (s32[1024]{0:T(1024)}, s32[1024]{0:T(1024)S(1)}, u32[]{:S(2)}) copy-start(s32[1024]{0:T(1024)S(1)} %pad_clamp_fusion.2) | copy-start | bytes 12292
  678.9 481.1 %copy-start.84 = (s32[1024]{0:T(1024)}, s32[1024]{0:T(1024)S(1)}, u32[]{:S(2)}) copy-start(s32[1024]{0:T(1024)S(1)} %pad_clamp_fusion.9) | copy-start | bytes 12292
  678.9 452.8 %copy-start.88 = (s32[1024]{0:T(1024)}, s32[1024]{0:T(1024)S(1)}, u32[]{:S(2)}) copy-start(s32[1024]{0:T(1024)S(1)} %pad_clamp_fusion.7) | copy-start | bytes 12292
  679.0 424.2 %copy-start.92 = (s32[1024]{0:T(1024)}, s32[1024]{0:T(1024)S(1)}, u32[]{:S(2)}) copy-start(s32[1024]{0:T(1024)S(1)} %pad_clamp_fusion.5) | copy-start | bytes 12292
  679.0 395.9 %copy-start.94 = (s32[1024]{0:T(1024)}, s32[1024]{0:T(1024)S(1)}, u32[]{:S(2)}) copy-start(s32[1024]{0:T(1024)S(1)} %pad_clamp_fusion.3) | copy-start | bytes 12292
  679.0 495.0 %copy-start.96 = (pred[512]{0:T(512)(128)(4,1)}, pred[512]{0:T(512)(128)(4,1)S(1)}, u32[]{:S(2)}) copy-start(pred[512]{0:T(512)(128)(4,1)S(1)} %get-tuple-element.113) | copy-start | bytes 1540
  679.0 495.0 %copy-start.98 = (pred[512]{0:T(512)(128)(4,1)}, pred[512]{0:T(512)(128)(4,1)S(1)}, u32[]{:S(2)}) copy-start(pred[512]{0:T(512)(128)(4,1)S(1)} %get-tuple-element.114) | copy-start | bytes 1540
  679.1 495.0 %copy-start.100 = (pred[512]{0:T(512)(128)(4,1)}, pred[512]{0:T(512)(128)(4,1)S(1)}, u32[]{:S(2)}) copy-start(pred[512]{0:T(512)(128)(4,1)S(1)} %get-tuple-element.115) | copy-start | bytes 1540
  679.1 495.0 %copy-start.102 = (pred[512]{0:T(512)(128)(4,1)}, pred[512]{0:T(512)(128)(4,1)S(1)}, u32[]{:S(2)}) copy-start(pred[512]{0:T(512)(128)(4,1)S(1)} %get-tuple-element.116) | copy-start | bytes 1540
  679.1 495.0 %copy-start.104 = (pred[512]{0:T(512)(128)(4,1)}, pred[512]{0:T(512)(128)(4,1)S(1)}, u32[]{:S(2)}) copy-start(pred[512]{0:T(512)(128)(4,1)S(1)} %get-tuple-element.117) | copy-start | bytes 1540
  679.1 495.0 %copy-start.106 = (pred[512]{0:T(512)(128)(4,1)}, pred[512]{0:T(512)(128)(4,1)S(1)}, u32[]{:S(2)}) copy-start(pred[512]{0:T(512)(128)(4,1)S(1)} %get-tuple-element.118) | copy-start | bytes 1540
  679.1 495.0 %copy-start.108 = (pred[512]{0:T(512)(128)(4,1)}, pred[512]{0:T(512)(128)(4,1)S(1)}, u32[]{:S(2)}) copy-start(pred[512]{0:T(512)(128)(4,1)S(1)} %get-tuple-element.119) | copy-start | bytes 1540
  679.2 495.0 %copy-start.110 = (pred[512]{0:T(512)(128)(4,1)}, pred[512]{0:T(512)(128)(4,1)S(1)}, u32[]{:S(2)}) copy-start(pred[512]{0:T(512)(128)(4,1)S(1)} %get-tuple-element.120) | copy-start | bytes 1540
  1174.1 20.0 copy-start.65
  1193.8 24.4 copy-start.50
  1194.1 24.2 copy-start.53
  1194.1 24.3 copy-start.64
  2094.6 8.1 copy-start.91
  2102.7 13.2 copy-start.95
  2115.9 14.3 copy-start.87
  2130.2 14.0 copy-start.93
  2144.2 14.1 copy-start.83
  2158.3 14.3 copy-start.89
  2172.6 14.1 copy-start.81
  2186.7 14.4 copy-start.85
  2201.1 14.1 copy-start.97
  2201.1 14.1 copy-start.99
  2201.1 14.1 copy-start.101
  2201.1 14.1 copy-start.103
  2201.1 14.1 copy-start.105
  2201.1 14.1 copy-start.107
  2201.2 14.1 copy-start.109
  2201.2 14.1 copy-start.111
  2223.8 141.4 %reduce-scatter.14.cloned.1.call-start = ((), (), s32[]{:S(2)}) async-start(), calls=%async_computation.15 | async-start | bytes 73728 | tf_op jit(solution)/shard_map/reduce_scatter | solution.py:263
  2226.4 226.9 %all-reduce.23.cloned.1.call-start = ((), (), s32[]{:S(2)}) async-start(), calls=%async_computation.16 | async-start | bytes 8388608 | tf_op jit(solution)/shard_map/psum | solution.py:155
  2226.5 80.7 %copy-start.49 = (bf16[2048,16]{0,1:T(8,128)(2,1)S(1)}, bf16[2048,16]{0,1:T(8,128)(2,1)}, u32[]{:S(2)}) copy-start(bf16[2048,16]{0,1:T(8,128)(2,1)} %param.30) | copy-start | bytes 196612
  2226.5 80.7 %copy-start.67 = (f32[2048]{0:T(1024)S(1)}, f32[2048]{0:T(1024)}, u32[]{:S(2)}) copy-start(f32[2048]{0:T(1024)} %param.29) | copy-start | bytes 24580
  2226.5 80.7 %copy-start.77 = (f32[512]{0:T(512)S(1)}, f32[512]{0:T(512)}, u32[]{:S(2)}) copy-start(f32[512]{0:T(512)} %copy-done.76) | copy-start | bytes 6148
  2236.5 75.5 %copy-start.14 = (bf16[512,2048]{1,0:T(8,128)(2,1)S(1)}, bf16[512,2048]{1,0:T(8,128)(2,1)}, u32[]{:S(2)}) copy-start(bf16[512,2048]{1,0:T(8,128)(2,1)} %param.21) | copy-start | bytes 6291460
  2318.7 10.4 copy-start.47
  2332.0 6.0 copy-start.11
  2332.0 193.5 %reduce-scatter.12.cloned.1.call-start = ((), (), s32[]{:S(2)}) async-start(), calls=%async_computation.14 | async-start | bytes 2359296 | tf_op jit(solution)/shard_map/reduce_scatter | solution.py:260
  2337.9 28.6 %copy-start.30 = (bf16[512,4,128]{0,2,1:T(8,128)(2,1)S(1)}, bf16[512,4,128]{0,2,1:T(8,128)(2,1)}, u32[]{:S(2)}) copy-start(bf16[512,4,128]{0,2,1:T(8,128)(2,1)} %copy-done.29) | copy-start | bytes 1572868
  2337.9 258.7 %reduce-scatter.10.cloned.1.call-start = ((), (), s32[]{:S(2)}) async-start(), calls=%async_computation.13 | async-start | bytes 2359296 | tf_op jit(solution)/shard_map/reduce_scatter | solution.py:257
  2342.0 325.8 %reduce-scatter.6.cloned.1.call-start = ((), (), s32[]{:S(2)}) async-start(), calls=%async_computation.11 | async-start | bytes 2359296 | tf_op jit(solution)/shard_map/reduce_scatter | solution.py:251
  2369.4 369.4 %reduce-scatter.8.cloned.1.call-start = ((), (), s32[]{:S(2)}) async-start(), calls=%async_computation.12 | async-start | bytes 2359296 | tf_op jit(solution)/shard_map/reduce_scatter | solution.py:254
  2478.5 15.9 copy-start.42
  2500.0 240.6 %copy-start.1 = (bf16[2,256,2048]{2,1,0:T(8,128)(2,1)S(1)}, bf16[2,256,2048]{2,1,0:T(8,128)(2,1)}, u32[]{:S(2)}) copy-start(bf16[2,256,2048]{2,1,0:T(8,128)(2,1)} %param.33) | copy-start | bytes 6291460
  (63 other events, 141.9 us)
Sparse Core Ops, SparseCore 0:
  28.8 88.1 all-reduce.18
  2223.9 83.1 all-reduce.20
  2310.3 54.8 reduce-scatter.13
  2368.7 84.5 all-reduce.22
  2456.7 68.7 reduce-scatter.11
  2528.9 67.6 reduce-scatter.9
  2600.1 67.6 reduce-scatter.5
  2671.3 67.3 reduce-scatter.7
where the time goes:
time: 2760 us; the launch traced here: 2750 us
  blocking collectives  1270 us (46%)
  waiting for transfers between devices  800 us (29%)
  local copies, waits for them, and re-layouts  420 us (15%)
  matrix products  130 us (5%)
  other arithmetic  99.7 us (4%)
    all_to_all x1, blocking collectives, on_device(): lax.all_to_all(send_buf, 'expert', split_axis=0, concat_axis=0, tiled=True)  413 us
    all_to_all x1, blocking collectives, on_device(): lax.all_to_all(grad_buf.reshape(expert_ranks, local_experts, capacity, mo...  412 us
    all_to_all x1, blocking collectives, on_device(): lax.all_to_all(dslot_in, 'expert', split_axis=0, concat_axis=0, tiled=True)  411 us
    all_to_all x1, waiting for transfers between devices, on_device(): lax.all_to_all(partial_out, 'expert', split_axis=0, concat_axis=0, tiled=...  362 us
    gather x8, local copies, waits for them, and re-layouts, on_device(): picked = jnp.take(returned, slot_ids[:, rank_k], axis=0)  113 us
    gather x8, local copies, waits for them, and re-layouts, on_device(): jnp.take(came_back, slot_ids[:, rank_k], axis=0)  112 us
    psum x1, waiting for transfers between devices, on_device(): dnormed_exp, dgate_all = lax.psum((dnormed_part, dgate_part), 'tensor')  70.6 us
    reduce_scatter x1, waiting for transfers between devices, on_device(): lax.psum_scatter(q_grad.astype(jnp.bfloat16), 'expert', scatter_dimension...  69.4 us
  transfers between devices with their start and end apart: 9, of which 9 were waited for; matrix products, arithmetic and copies ran while one was open for 6% of the time, Pallas kernels for 0%

commit v1 on v0

--- a/solution.py
+++ b/solution.py
@@ -1,3 +1,4 @@
+import functools
 import jax
 import jax.numpy as jnp
 from jax import lax
@@ -6,6 +7,39 @@
 epsilon = 1e-06
 rope_base = 10000.0
 masked_score = -1e30
+
+
+def local_data_trace(mat, ndim_at, message):
+    heard, view_out = (mat.shape[:ndim_at], mat.shape[ndim_at + 1 :])
+    return jnp.moveaxis(mat.reshape(*heard, message, -1, *view_out), ndim_at, 0)
+
+
+def feed_ratios_on(xx, d_out):
+    part_next = list(xx.shape[1:])
+    part_next[d_out] *= xx.shape[0]
+    return jnp.moveaxis(xx, 0, d_out).reshape(part_next)
+
+
+def store_axis_part_here(tile_in, which_axis, point, incoming_x):
+    block_last, r2 = (lax.axis_size(which_axis), lax.axis_index(which_axis))
+    local_next = local_data_trace(tile_in, point, block_last)
+    line_up = [local_next[r2]]
+    kk = 1
+    while kk < block_last:
+        piece_now = local_next[r2 ^ kk]
+        line_up.append(
+            lax.ppermute(
+                piece_now,
+                axis_name=which_axis,
+                perm=[(to_i, to_i ^ kk) for to_i in range(block_last)],
+            )
+        )
+        kk = kk + 1
+    local_next = jnp.stack(line_up, axis=0)[r2 ^ jnp.arange(block_last)]
+    return feed_ratios_on(local_next, incoming_x)
+
+
+time_the_zone = functools.partial(store_axis_part_here, which_axis="expert", point=0, incoming_x=0)
 
 
 def rms_scale(values):
@@ -181,9 +215,7 @@
         "secf,edf->secd", djoint, gate_up, preferred_element_type=jnp.float32
     ).astype(jnp.bfloat16)
     dnormed_part = jnp.zeros((num_tokens, model_width), jnp.float32)
-    came_back = lax.all_to_all(dslot_in, "expert", split_axis=0, concat_axis=0, tiled=True).reshape(
-        all_experts * capacity, model_width
-    )
+    came_back = time_the_zone(dslot_in).reshape(all_experts * capacity, model_width)
     came_back = jnp.concatenate([came_back, zero_row], 0)
     for rank_k in range(num_picks):
         dnormed_part = dnormed_part + jnp.take(came_back, slot_ids[:, rank_k], axis=0)

time: 2760 us -> 2800 us (1.014)
  blocking collectives: 1270 us -> 452 us
  waiting for transfers between devices: 800 us -> 1600 us
  local copies, waits for them, and re-layouts: 420 us -> 457 us
    all_to_all x2 -> x0, blocking collectives: 823 us -> none  [the longest x1 412 us: on_device(): lax.all_to_all(grad_buf.reshape(expert_ranks, local_experts, capacity, mo...]
    all_to_all x0 -> x1, waiting for transfers between devices: none -> 406 us  [on_device(): lax.all_to_all(grad_buf.reshape(expert_ranks, local_experts, capacity, mo...]
    ppermute x0 -> x7, waiting for transfers between devices: none -> 291 us  [store_axis_part_here(): lax.ppermute(piece_now, axis_name=which_axis, perm=[(to_i, to_i ^ kk) for...]
    psum x1, waiting for transfers between devices: 70.6 us -> 170 us  [on_device(): dnormed_exp, dgate_all = lax.psum((dnormed_part, dgate_part), 'tensor')]
  transfers between devices with their start and end apart: 9 -> 17, of which waited for: 9 -> 14; matrix products, arithmetic and copies ran while one was open for 6% -> 6% of each run, Pallas kernels for 0% -> 0%
where the time goes in v1:
time: 2800 us; the launch traced here: 2790 us
  waiting for transfers between devices  1600 us (57%)
  local copies, waits for them, and re-layouts  457 us (16%)
  blocking collectives  452 us (16%)
  matrix products  130 us (5%)
  other arithmetic  116 us (4%)
    all_to_all x1, blocking collectives, on_device(): lax.all_to_all(send_buf, 'expert', split_axis=0, concat_axis=0, tiled=True)  413 us
    all_to_all x1, waiting for transfers between devices, on_device(): lax.all_to_all(grad_buf.reshape(expert_ranks, local_experts, capacity, mo...  406 us
    all_to_all x1, waiting for transfers between devices, on_device(): lax.all_to_all(partial_out, 'expert', split_axis=0, concat_axis=0, tiled=...  363 us
    ppermute x7, waiting for transfers between devices, store_axis_part_here(): lax.ppermute(piece_now, axis_name=which_axis, perm=[(to_i, to_i ^ kk) for...  291 us
    psum x1, waiting for transfers between devices, on_device(): dnormed_exp, dgate_all = lax.psum((dnormed_part, dgate_part), 'tensor')  170 us
    gather x8, local copies, waits for them, and re-layouts, on_device(): picked = jnp.take(returned, slot_ids[:, rank_k], axis=0)  113 us
    gather x8, local copies, waits for them, and re-layouts, on_device(): jnp.take(came_back, slot_ids[:, rank_k], axis=0)  112 us
    reduce_scatter x1, waiting for transfers between devices, on_device(): lax.psum_scatter(q_grad.astype(jnp.bfloat16), 'expert', scatter_dimension...  69.4 us
  transfers between devices with their start and end apart: 17, of which 14 were waited for; matrix products, arithmetic and copies ran while one was open for 6% of the time, Pallas kernels for 0%

profile of v1, /device:TPU:0, one launch (start us, length us, event | category | flops | bytes accessed | tf_op | source)
XLA Modules:
  0.0 2794.2 jit_solution(17151156353194940265)
XLA Ops:
  29.7 4.8 reduce-window.6
  36.8 15.5 scatter_custom_fusion
  53.2 63.9 %all-reduce.19.cloned.1.call-done = f32[512,2048]{1,0:T(8,128)} async-done(((f32[512,2048]{1,0:T(8,128)}), f32[512,2048]{1,0:T(8,128)}) %all-reduce.19.cloned.1.call-update) | async-done | bytes 4194320 | tf_op jit(solution)/shard_map/psum | solution.py:153
  124.2 36.9 %gather_fusion = bf16[4608,2048]{1,0:T(8,128)(2,1)} fusion(bf16[513,2048]{1,0:T(8,128)(2,1)} %concatenate.39, s32[5120]{0:T(1024)S(1)} %get-tuple-element.129), kind=kCustom, calls=%fused_computation.16 | custom fusion | bytes 37767168 | tf_op jit(solution)/shard_map/jit(_take)/gather | solution.py:165
  161.1 9.7 broadcast_select_fusion
  170.9 413.4 %all_to_all.15 = bf16[8,2,288,2048]{3,2,1,0:T(8,128)(2,1)} all-to-all(bf16[8,2,288,2048]{3,2,1,0:T(8,128)(2,1)S(1)} %broadcast_select_fusion), channel_id=1, replica_groups=mesh['expert'=8,'tensor'=4] {'expert'}, dimensions={0} | all-to-all | bytes 37748736 | tf_op jit(solution)/shard_map/all_to_all | solution.py:168
  584.3 16.5 fusion.42
  600.7 4.5 multiply_convert_fusion.1
  605.2 9.1 convert_bitcast_fusion
  614.3 16.9 copy.135
  631.3 6.1 all-to-all-start.1
  641.5 36.2 %gather_fusion.2 = f32[4608,2048]{1,0:T(8,128)} fusion(f32[513,2048]{1,0:T(8,128)} %concatenate.42, s32[5120]{0:T(1024)S(1)} %get-tuple-element.129), kind=kCustom, calls=%fused_computation.18 | custom fusion | bytes 75515904 | tf_op jit(solution)/shard_map/jit(_take)/gather | solution.py:195
  681.6 362.6 %all-to-all-done.1 = bf16[8,2,288,2048]{3,2,1,0:T(8,128)(2,1)} async-done(((bf16[8,2,288,2048]{3,2,1,0:T(8,128)(2,1)}), bf16[8,2,288,2048]{3,2,1,0:T(8,128)(2,1)}, u32[]{:S(2)}, u32[]{:S(2)}) %all-to-all-start.1) | async-done | bytes 18874400 | tf_op jit(solution)/shard_map/all_to_all | solution.py:181
  1044.2 16.9 concatenate.40
  1061.2 14.0 gather_fusion.12
  1075.2 14.5 gather_fusion.11
  1089.7 14.1 gather_fusion.10
  1103.8 14.2 gather_fusion.9
  1118.0 14.0 gather_fusion.8
  1132.1 14.0 gather_fusion.7
  1146.1 14.2 gather_fusion.6
  1160.3 14.1 gather_fusion.5
  1174.5 8.9 fusion.41
  1183.4 10.1 psum.52
  1194.5 24.1 gather_fusion.1
  1218.8 21.3 multiply_convert_fusion
  1240.1 5.9 all-to-all-start.2
  1246.1 406.4 %all-to-all-done.2 = bf16[8,2,288,2048]{3,2,1,0:T(8,128)(2,1)} async-done(((bf16[8,2,288,2048]{3,2,1,0:T(8,128)(2,1)}), bf16[8,2,288,2048]{3,2,1,0:T(8,128)(2,1)}, u32[]{:S(2)}, u32[]{:S(2)}) %all-to-all-start.2) | async-done | bytes 18874400 | tf_op jit(solution)/shard_map/all_to_all | solution.py:196
  1652.5 14.4 fusion.12
  1666.9 15.8 convolution_convert_fusion
  1682.6 12.0 dynamic-slice_bitcast_fusion
  1704.0 43.1 %collective-permute-done = bf16[1,2,288,2048]{3,2,1,0:T(8,128)(2,1)} collective-permute-done((bf16[1,2,288,2048]{3,2,1,0:T(8,128)(2,1)}, bf16[1,2,288,2048]{3,2,1,0:T(8,128)(2,1)}, u32[]{:S(2)}, u32[]{:S(2)}) %collective-permute-start) | collective-permute-done | bytes 2359328 | tf_op jit(solution)/shard_map/ppermute | solution.py:31
  1752.3 97.2 %collective-permute-done.1 = bf16[1,2,288,2048]{3,2,1,0:T(8,128)(2,1)} collective-permute-done((bf16[1,2,288,2048]{3,2,1,0:T(8,128)(2,1)}, bf16[1,2,288,2048]{3,2,1,0:T(8,128)(2,1)}, u32[]{:S(2)}, u32[]{:S(2)}) %collective-permute-start.1) | collective-permute-done | bytes 2359328 | tf_op jit(solution)/shard_map/ppermute | solution.py:31
  1852.5 45.3 %collective-permute-done.2 = bf16[1,2,288,2048]{3,2,1,0:T(8,128)(2,1)} collective-permute-done((bf16[1,2,288,2048]{3,2,1,0:T(8,128)(2,1)}, bf16[1,2,288,2048]{3,2,1,0:T(8,128)(2,1)}, u32[]{:S(2)}, u32[]{:S(2)}) %collective-permute-start.2) | collective-permute-done | bytes 2359328 | tf_op jit(solution)/shard_map/ppermute | solution.py:31
  1901.4 105.7 %collective-permute-done.4 = bf16[1,2,288,2048]{3,2,1,0:T(8,128)(2,1)S(1)} collective-permute-done((bf16[1,2,288,2048]{3,2,1,0:T(8,128)(2,1)}, bf16[1,2,288,2048]{3,2,1,0:T(8,128)(2,1)S(1)}, u32[]{:S(2)}, u32[]{:S(2)}) %collective-permute-start.4) | collective-permute-done | bytes 2359328 | tf_op jit(solution)/shard_map/ppermute | solution.py:31
  2007.7 6.9 slice_bitcast_fusion.1
  2014.6 8.8 gather_fusion.3
  2023.4 8.9 gather_fusion.4
  2032.3 9.4 pad_maximum_fusion
  2041.6 8.2 concatenate.44
  2049.9 13.2 gather_fusion.20
  2063.1 14.0 gather_fusion.19
  2077.2 14.5 gather_fusion.18
  2091.7 14.1 gather_fusion.17
  2105.7 14.3 gather_fusion.16
  2120.0 14.1 gather_fusion.15
  2134.1 14.1 gather_fusion.14
  2148.2 14.1 gather_fusion.13
  2162.4 8.4 convert_add_fusion.2
  2173.6 9.8 fusion.29
  2183.4 170.3 %all-reduce.21.cloned.1.call-done = f32[512,2048]{1,0:T(8,128)} async-done(((f32[512,2048]{1,0:T(8,128)}), f32[512,2048]{1,0:T(8,128)}) %all-reduce.21.cloned.1.call-update) | async-done | bytes 4194320 | tf_op jit(solution)/shard_map/psum | solution.py:222
  2353.7 4.9 multiply_reduce_fusion
  2379.6 4.8 convolution_convert_fusion.1
  2390.5 21.3 reduce-scatter.14.cloned.1.call-done
  2416.0 18.0 fusion.17
  2436.9 11.3 fusion.45
  2448.1 51.7 %all-reduce.23.cloned.1.call-done = (bf16[512,2048]{1,0:T(8,128)(2,1)}, bf16[512,2048]{1,0:T(8,128)(2,1)}) async-done(((bf16[512,2048]{1,0:T(8,128)(2,1)}, bf16[512,2048]{1,0:T(8,128)(2,1)}), (bf16[512,2048]{1,0:T(8,128)(2,1)}, bf16[512,2048]{1,0:T(8,128)(2,1)})) %all-reduce.23.cloned.1.call-update) | async-done | bytes 4194320 | tf_op jit(solution)/shard_map/psum | solution.py:189
  2502.8 22.2 all-reduce.12
  2525.1 7.6 fusion.92
  2532.7 6.0 all-reduce.13
  2549.9 22.2 reduce-scatter.12.cloned.1.call-done
  2573.9 69.3 %reduce-scatter.10.cloned.1.call-done = bf16[256,512]{1,0:T(8,128)(2,1)} async-done(((bf16[2048,512]{1,0:T(8,128)(2,1)}), bf16[256,512]{1,0:T(8,128)(2,1)}) %reduce-scatter.10.cloned.1.call-update) | async-done | bytes 262160 | tf_op jit(solution)/shard_map/reduce_scatter | solution.py:289
  2645.0 69.4 %reduce-scatter.6.cloned.1.call-done = bf16[256,512]{1,0:T(8,128)(2,1)} async-done(((bf16[2048,512]{1,0:T(8,128)(2,1)}), bf16[256,512]{1,0:T(8,128)(2,1)}) %reduce-scatter.6.cloned.1.call-update) | async-done | bytes 262160 | tf_op jit(solution)/shard_map/reduce_scatter | solution.py:283
  2716.2 69.1 %reduce-scatter.8.cloned.1.call-done = bf16[256,512]{1,0:T(8,128)(2,1)} async-done(((bf16[2048,512]{1,0:T(8,128)(2,1)}), bf16[256,512]{1,0:T(8,128)(2,1)}) %reduce-scatter.8.cloned.1.call-update) | async-done | bytes 262160 | tf_op jit(solution)/shard_map/reduce_scatter | solution.py:286
  (388 shorter events, 119.3 us)
Async XLA Ops:
  7.2 598.1 %copy-start = (bf16[2,256,2048]{2,1,0:T(8,128)(2,1)S(1)}, bf16[2,256,2048]{2,1,0:T(8,128)(2,1)}, u32[]{:S(2)}) copy-start(bf16[2,256,2048]{2,1,0:T(8,128)(2,1)} %param.33) | copy-start | bytes 6291460
  7.2 109.9 %all-reduce.19.cloned.1.call-start = ((), (), s32[]{:S(2)}) async-start(), calls=%async_computation.8 | async-start | bytes 8388608 | tf_op jit(solution)/shard_map/psum | solution.py:153
  52.5 68.1 %copy-start.54 = (s32[8,2,288]{2,1,0:T(2,128)}, s32[8,2,288]{2,1,0:T(2,128)S(1)}, u32[]{:S(2)}) copy-start(s32[8,2,288]{2,1,0:T(2,128)S(1)} %slice.99) | copy-start | bytes 55300
  53.2 107.9 %copy-start.65 = (pred[8,2,288]{2,1,0:T(4,128)(4,1)}, pred[8,2,288]{2,1,0:T(4,128)(4,1)S(1)}, u32[]{:S(2)}) copy-start(pred[8,2,288]{2,1,0:T(4,128)(4,1)S(1)} %compare_and_fusion) | copy-start | bytes 13828
  53.2 67.4 %copy-start.68 = (f32[2048]{0:T(1024)S(1)}, f32[2048]{0:T(1024)}, u32[]{:S(2)}) copy-start(f32[2048]{0:T(1024)} %param.29) | copy-start | bytes 24580
  631.3 413.0 %all-to-all-start.1 = ((bf16[8,2,288,2048]{3,2,1,0:T(8,128)(2,1)}), bf16[8,2,288,2048]{3,2,1,0:T(8,128)(2,1)}, u32[]{:S(2)}, u32[]{:S(2)}) async-start(bf16[8,2,288,2048]{3,2,1,0:T(8,128)(2,1)} %copy.135), calls=%async_computation.1 | async-start | bytes 37748736 | tf_op jit(solution)/shard_map/all_to_all | solution.py:181
  641.5 36.2 %copy-start.13 = (s32[512,8]{1,0:T(8,128)S(1)}, s32[512,8]{1,0:T(8,128)}, u32[]{:S(2)}) copy-start(s32[512,8]{1,0:T(8,128)} %get-tuple-element.76) | copy-start | bytes 49156
  641.5 37.7 %copy-start.50 = (bf16[2048,16]{0,1:T(8,128)(2,1)S(1)}, bf16[2048,16]{0,1:T(8,128)(2,1)}, u32[]{:S(2)}) copy-start(bf16[2048,16]{0,1:T(8,128)(2,1)} %param.30) | copy-start | bytes 196612
  678.9 467.2 %copy-start.82 = (s32[1024]{0:T(1024)}, s32[1024]{0:T(1024)S(1)}, u32[]{:S(2)}) copy-start(s32[1024]{0:T(1024)S(1)} %pad_clamp_fusion.9) | copy-start | bytes 12292
  678.9 439.1 %copy-start.84 = (s32[1024]{0:T(1024)}, s32[1024]{0:T(1024)S(1)}, u32[]{:S(2)}) copy-start(s32[1024]{0:T(1024)S(1)} %pad_clamp_fusion.7) | copy-start | bytes 12292
  678.9 410.8 %copy-start.88 = (s32[1024]{0:T(1024)}, s32[1024]{0:T(1024)S(1)}, u32[]{:S(2)}) copy-start(s32[1024]{0:T(1024)S(1)} %pad_clamp_fusion.5) | copy-start | bytes 12292
  679.0 382.2 %copy-start.92 = (s32[1024]{0:T(1024)}, s32[1024]{0:T(1024)S(1)}, u32[]{:S(2)}) copy-start(s32[1024]{0:T(1024)S(1)} %pad_clamp_fusion.3) | copy-start | bytes 12292
  679.0 481.3 %copy-start.86 = (s32[1024]{0:T(1024)}, s32[1024]{0:T(1024)S(1)}, u32[]{:S(2)}) copy-start(s32[1024]{0:T(1024)S(1)} %pad_clamp_fusion.10) | copy-start | bytes 12292
  679.0 453.0 %copy-start.90 = (s32[1024]{0:T(1024)}, s32[1024]{0:T(1024)S(1)}, u32[]{:S(2)}) copy-start(s32[1024]{0:T(1024)S(1)} %pad_clamp_fusion.8) | copy-start | bytes 12292
  679.0 424.8 %copy-start.94 = (s32[1024]{0:T(1024)}, s32[1024]{0:T(1024)S(1)}, u32[]{:S(2)}) copy-start(s32[1024]{0:T(1024)S(1)} %pad_clamp_fusion.6) | copy-start | bytes 12292
  679.1 396.1 %copy-start.96 = (s32[1024]{0:T(1024)}, s32[1024]{0:T(1024)S(1)}, u32[]{:S(2)}) copy-start(s32[1024]{0:T(1024)S(1)} %pad_clamp_fusion.4) | copy-start | bytes 12292
  679.1 495.3 %copy-start.98 = (pred[512]{0:T(512)(128)(4,1)}, pred[512]{0:T(512)(128)(4,1)S(1)}, u32[]{:S(2)}) copy-start(pred[512]{0:T(512)(128)(4,1)S(1)} %get-tuple-element.120) | copy-start | bytes 1540
  679.1 495.3 %copy-start.100 = (pred[512]{0:T(512)(128)(4,1)}, pred[512]{0:T(512)(128)(4,1)S(1)}, u32[]{:S(2)}) copy-start(pred[512]{0:T(512)(128)(4,1)S(1)} %get-tuple-element.121) | copy-start | bytes 1540
  679.1 495.3 %copy-start.102 = (pred[512]{0:T(512)(128)(4,1)}, pred[512]{0:T(512)(128)(4,1)S(1)}, u32[]{:S(2)}) copy-start(pred[512]{0:T(512)(128)(4,1)S(1)} %get-tuple-element.122) | copy-start | bytes 1540
  679.1 495.3 %copy-start.104 = (pred[512]{0:T(512)(128)(4,1)}, pred[512]{0:T(512)(128)(4,1)S(1)}, u32[]{:S(2)}) copy-start(pred[512]{0:T(512)(128)(4,1)S(1)} %get-tuple-element.123) | copy-start | bytes 1540
  679.2 495.3 %copy-start.106 = (pred[512]{0:T(512)(128)(4,1)}, pred[512]{0:T(512)(128)(4,1)S(1)}, u32[]{:S(2)}) copy-start(pred[512]{0:T(512)(128)(4,1)S(1)} %get-tuple-element.124) | copy-start | bytes 1540
  679.2 495.3 %copy-start.108 = (pred[512]{0:T(512)(128)(4,1)}, pred[512]{0:T(512)(128)(4,1)S(1)}, u32[]{:S(2)}) copy-start(pred[512]{0:T(512)(128)(4,1)S(1)} %get-tuple-element.125) | copy-start | bytes 1540
  679.2 495.2 %copy-start.110 = (pred[512]{0:T(512)(128)(4,1)}, pred[512]{0:T(512)(128)(4,1)S(1)}, u32[]{:S(2)}) copy-start(pred[512]{0:T(512)(128)(4,1)S(1)} %get-tuple-element.126) | copy-start | bytes 1540
  679.2 495.2 %copy-start.112 = (pred[512]{0:T(512)(128)(4,1)}, pred[512]{0:T(512)(128)(4,1)S(1)}, u32[]{:S(2)}) copy-start(pred[512]{0:T(512)(128)(4,1)S(1)} %get-tuple-element.127) | copy-start | bytes 1540
  1174.5 20.0 copy-start.67
  1194.2 24.4 copy-start.52
  1194.5 24.2 copy-start.55
  1194.5 24.3 copy-start.66
  1240.1 412.4 %all-to-all-start.2 = ((bf16[8,2,288,2048]{3,2,1,0:T(8,128)(2,1)}), bf16[8,2,288,2048]{3,2,1,0:T(8,128)(2,1)}, u32[]{:S(2)}, u32[]{:S(2)}) async-start(bf16[8,2,288,2048]{3,2,1,0:T(8,128)(2,1)} %multiply_convert_fusion), calls=%async_computation.2 | async-start | bytes 37748736 | tf_op jit(solution)/shard_map/all_to_all | solution.py:196
  1246.0 1107.7 %all-reduce.21.cloned.1.call-start = ((), (), s32[]{:S(2)}) async-start(), calls=%async_computation.9 | async-start | bytes 8388608 | tf_op jit(solution)/shard_map/psum | solution.py:222
  1694.7 52.4 %collective-permute-start = (bf16[1,2,288,2048]{3,2,1,0:T(8,128)(2,1)}, bf16[1,2,288,2048]{3,2,1,0:T(8,128)(2,1)}, u32[]{:S(2)}, u32[]{:S(2)}) collective-permute-start(bf16[1,2,288,2048]{3,2,1,0:T(8,128)(2,1)} %get-tuple-element.60), channel_id=1, source_target_pairs={{0,4},{4,0},{8,12},{12,8},{16,20},{20,16},{24,28},{28,24},{1,5},{5... | collective-permute-start | bytes 7077896 | tf_op jit(solution)/shard_map/ppermute | solution.py:31
  1696.2 153.4 %collective-permute-start.1 = (bf16[1,2,288,2048]{3,2,1,0:T(8,128)(2,1)}, bf16[1,2,288,2048]{3,2,1,0:T(8,128)(2,1)}, u32[]{:S(2)}, u32[]{:S(2)}) collective-permute-start(bf16[1,2,288,2048]{3,2,1,0:T(8,128)(2,1)} %get-tuple-element.59), channel_id=1, source_target_pairs={{0,8},{4,12},{8,0},{12,4},{16,24},{20,28},{24,16},{28,20},{1,9},{5... | collective-permute-start | bytes 7077896 | tf_op jit(solution)/shard_map/ppermute | solution.py:31
  1696.2 201.5 %collective-permute-start.2 = (bf16[1,2,288,2048]{3,2,1,0:T(8,128)(2,1)}, bf16[1,2,288,2048]{3,2,1,0:T(8,128)(2,1)}, u32[]{:S(2)}, u32[]{:S(2)}) collective-permute-start(bf16[1,2,288,2048]{3,2,1,0:T(8,128)(2,1)} %get-tuple-element.58), channel_id=1, source_target_pairs={{0,12},{4,8},{8,4},{12,0},{16,28},{20,24},{24,20},{28,16},{1,13},{... | collective-permute-start | bytes 7077896 | tf_op jit(solution)/shard_map/ppermute | solution.py:31
  1698.2 201.4 %collective-permute-start.3 = (bf16[1,2,288,2048]{3,2,1,0:T(8,128)(2,1)}, bf16[1,2,288,2048]{3,2,1,0:T(8,128)(2,1)}, u32[]{:S(2)}, u32[]{:S(2)}) collective-permute-start(bf16[1,2,288,2048]{3,2,1,0:T(8,128)(2,1)} %get-tuple-element.57), channel_id=1, source_target_pairs={{0,16},{4,20},{8,24},{12,28},{16,0},{20,4},{24,8},{28,12},{1,17},{... | collective-permute-start | bytes 7077896 | tf_op jit(solution)/shard_map/ppermute | solution.py:31
  1699.0 48.0 %copy-start.36 = (bf16[1,2,288,2048]{3,2,1,0:T(8,128)(2,1)S(1)}, bf16[1,2,288,2048]{3,2,1,0:T(8,128)(2,1)}, u32[]{:S(2)}) copy-start(bf16[1,2,288,2048]{3,2,1,0:T(8,128)(2,1)} %get-tuple-element.61) | copy-start | bytes 7077892
  1699.1 150.5 %copy-start.35 = (bf16[1,2,288,2048]{3,2,0,1:T(8,128)(2,1)S(1)}, bf16[1,2,288,2048]{3,2,0,1:T(8,128)(2,1)}, u32[]{:S(2)}) copy-start(bf16[1,2,288,2048]{3,2,0,1:T(8,128)(2,1)} %get-tuple-element.55) | copy-start | bytes 7077892
  1699.1 308.1 %collective-permute-start.4 = (bf16[1,2,288,2048]{3,2,1,0:T(8,128)(2,1)}, bf16[1,2,288,2048]{3,2,1,0:T(8,128)(2,1)S(1)}, u32[]{:S(2)}, u32[]{:S(2)}) collective-permute-start(bf16[1,2,288,2048]{3,2,1,0:T(8,128)(2,1)} %get-tuple-element.56), channel_id=1, source_target_pairs={{0,20},{4,16},{8,28},{12,24},{16,4},{20,0},{24,12},{28,8},{1,21},{... | collective-permute-start | bytes 7077896 | tf_op jit(solution)/shard_map/ppermute | solution.py:31
  1747.0 260.3 %collective-permute-start.5 = (bf16[1,2,288,2048]{3,2,1,0:T(8,128)(2,1)S(1)}, bf16[1,2,288,2048]{3,2,1,0:T(8,128)(2,1)S(1)}, u32[]{:S(2)}, u32[]{:S(2)}) collective-permute-start(bf16[1,2,288,2048]{3,2,1,0:T(8,128)(2,1)S(1)} %copy-done.36), channel_id=1, source_target_pairs={{0,24},{4,28},{8,16},{12,20},{16,8},{20,12},{24,0},{28,4},{1,25},{... | collective-permute-start | bytes 7077896 | tf_op jit(solution)/shard_map/ppermute | solution.py:31
  1849.6 157.9 %collective-permute-start.6 = (bf16[1,2,288,2048]{3,2,0,1:T(8,128)(2,1)S(1)}, bf16[1,2,288,2048]{3,2,0,1:T(8,128)(2,1)S(1)}, u32[]{:S(2)}, u32[]{:S(2)}) collective-permute-start(bf16[1,2,288,2048]{3,2,0,1:T(8,128)(2,1)S(1)} %copy-done.35), channel_id=1, source_target_pairs={{0,28},{4,24},{8,20},{12,16},{16,12},{20,8},{24,4},{28,0},{1,29},{... | collective-permute-start | bytes 7077896 | tf_op jit(solution)/shard_map/ppermute | solution.py:31
  2077.2 14.5 copy-start.95
  2091.7 14.1 copy-start.85
  2105.7 14.3 copy-start.91
  2120.0 14.1 copy-start.83
  2148.1 14.2 copy-start.99
  2148.1 14.2 copy-start.101
  2148.2 14.2 copy-start.103
  2148.2 14.2 copy-start.105
  2148.2 14.2 copy-start.107
  2148.2 14.2 copy-start.109
  2148.2 14.2 copy-start.111
  2148.2 14.2 copy-start.113
  2170.9 240.9 %reduce-scatter.14.cloned.1.call-start = ((), (), s32[]{:S(2)}) async-start(), calls=%async_computation.14 | async-start | bytes 73728 | tf_op jit(solution)/shard_map/reduce_scatter | solution.py:295
  2173.5 326.4 %all-reduce.23.cloned.1.call-start = ((), (), s32[]{:S(2)}) async-start(), calls=%async_computation.15 | async-start | bytes 8388608 | tf_op jit(solution)/shard_map/psum | solution.py:189
  2173.6 180.2 %copy-start.51 = (bf16[2048,16]{0,1:T(8,128)(2,1)S(1)}, bf16[2048,16]{0,1:T(8,128)(2,1)}, u32[]{:S(2)}) copy-start(bf16[2048,16]{0,1:T(8,128)(2,1)} %param.30) | copy-start | bytes 196612
  2173.6 180.2 %copy-start.69 = (f32[2048]{0:T(1024)S(1)}, f32[2048]{0:T(1024)}, u32[]{:S(2)}) copy-start(f32[2048]{0:T(1024)} %param.29) | copy-start | bytes 24580
  2173.6 180.2 %copy-start.79 = (f32[512]{0:T(512)S(1)}, f32[512]{0:T(512)}, u32[]{:S(2)}) copy-start(f32[512]{0:T(512)} %copy-done.78) | copy-start | bytes 6148
  2183.4 175.3 %copy-start.14 = (bf16[512,2048]{1,0:T(8,128)(2,1)S(1)}, bf16[512,2048]{1,0:T(8,128)(2,1)}, u32[]{:S(2)}) copy-start(bf16[512,2048]{1,0:T(8,128)(2,1)} %param.21) | copy-start | bytes 6291460
  2378.6 193.5 %reduce-scatter.12.cloned.1.call-start = ((), (), s32[]{:S(2)}) async-start(), calls=%async_computation.13 | async-start | bytes 2359296 | tf_op jit(solution)/shard_map/reduce_scatter | solution.py:292
  2384.5 28.6 %copy-start.30 = (bf16[512,4,128]{0,2,1:T(8,128)(2,1)S(1)}, bf16[512,4,128]{0,2,1:T(8,128)(2,1)}, u32[]{:S(2)}) copy-start(bf16[512,4,128]{0,2,1:T(8,128)(2,1)} %copy-done.29) | copy-start | bytes 1572868
  2384.5 258.7 %reduce-scatter.10.cloned.1.call-start = ((), (), s32[]{:S(2)}) async-start(), calls=%async_computation.12 | async-start | bytes 2359296 | tf_op jit(solution)/shard_map/reduce_scatter | solution.py:289
  2388.6 325.8 %reduce-scatter.6.cloned.1.call-start = ((), (), s32[]{:S(2)}) async-start(), calls=%async_computation.10 | async-start | bytes 2359296 | tf_op jit(solution)/shard_map/reduce_scatter | solution.py:283
  2416.0 369.4 %reduce-scatter.8.cloned.1.call-start = ((), (), s32[]{:S(2)}) async-start(), calls=%async_computation.11 | async-start | bytes 2359296 | tf_op jit(solution)/shard_map/reduce_scatter | solution.py:286
  2525.1 15.9 copy-start.44
  2546.6 240.6 %copy-start.1 = (bf16[2,256,2048]{2,1,0:T(8,128)(2,1)S(1)}, bf16[2,256,2048]{2,1,0:T(8,128)(2,1)}, u32[]{:S(2)}) copy-start(bf16[2,256,2048]{2,1,0:T(8,128)(2,1)} %param.33) | copy-start | bytes 6291460
  (73 other events, 244.5 us)
Sparse Core Ops, SparseCore 0:
  28.9 88.2 all-reduce.18
  2171.0 182.6 all-reduce.20
  2356.9 54.8 reduce-scatter.13
  2415.2 84.5 all-reduce.22
  2503.3 68.7 reduce-scatter.11
  2575.5 67.6 reduce-scatter.9
  2646.7 67.6 reduce-scatter.5
  2717.9 67.3 reduce-scatter.7
